TPU v7x, 256 devices: a whole 4x4x8 slice. The times are simulated.
256 devices in a mesh: lat: 8 (over z), slab: 32 (over x, y, core).
Axes of the slice: x: 4, y: 4, z: 8, core: 2. Of those that a mesh axis runs over, the one named last changes fastest.
Arguments:
- field_state: float32 [8, 128, 128, 5, 128], P('lat', 'slab'), may hold values from -6 to 6
- cotangent: float32 [8, 128, 128, 5, 128], P('lat', None, 'slab'), may hold values from -6 to 6
- vertical_weight: float32 [8, 128, 128, 128], P('lat', 'slab'), may hold values from 0 to 1
- diffusion_inverse: float32 [8, 5, 128, 128], P('lat'), as said below
- source_row: int32 [8, 32, 8, 32, 4], P('lat', 'slab'), may hold values from 0 to 383, as said below
- dest_slot: int32 [8, 32, 512], P('lat', 'slab'), may hold values from 0 to 1023, as said below
Outputs:
- tangent_out: float32 [8, 128, 128, 5, 128], P('lat', None, 'slab')
- adjoint_out: float32 [8, 128, 128, 5, 128], P('lat', 'slab')
Inputs may be any that keep to these rules, and one draw needn't show every extreme that they name: `source_row`: from one sender to one receiver at most 4 slots are used, the used ones first; unused slots hold 0. Every value is below (3) * 128. `dest_slot`: each device's arrival rows name distinct used slots, and every used slot aimed at that device is named once; some sender fills all 4 slots to a receiver in every draw. `diffusion_inverse`: dense matrices of order one.
All inputs are finite; a program needn't handle non-finite values.
Results may differ from a plain program's by a relative error of at most 0.00007.
Values sent between devices are 32-bit elements; how exact they have to be, the bound alone decides.
A program may use at most 128 MiB of HBM per device.

v0:
```python
import jax
import jax.numpy as jnp
from jax import lax
from jax.sharding import PartitionSpec as P


def select(table, values):
    return jnp.dot(
        table, values, precision=lax.Precision.HIGHEST, preferred_element_type=jnp.float32
    )


def select_back(table, values):
    return lax.dot_general(
        table,
        values,
        (((0,), (0,)), ((), ())),
        precision=lax.Precision.HIGHEST,
        preferred_element_type=jnp.float32,
    )


def body(field_state, cotangent, vertical_weight, diffusion_inverse, source_row, dest_slot):
    highest = lax.Precision.HIGHEST
    levels_here = field_state.shape[1]
    blocks = field_state.shape[2]
    fields = field_state.shape[3]
    width = field_state.shape[4]
    row_total = levels_here * blocks
    low_total = row_total - blocks
    flat_width = fields * width
    inverse = diffusion_inverse[0]
    level_rows = field_state.reshape(row_total, flat_width)
    weights = vertical_weight.reshape(row_total, width)
    lower_idx = source_row[0, 0]
    slots = dest_slot[0, 0]
    slot_total = lower_idx.size
    lower_flat = lower_idx.reshape(-1)
    row_ids = jnp.arange(low_total, dtype=jnp.int32)
    slot_ids = jnp.arange(slot_total, dtype=jnp.int32)
    source_table = (lower_flat[:, None] == row_ids[None, :]).astype(jnp.float32)
    arrival_table = (slots[:, None] == slot_ids[None, :]).astype(jnp.float32)
    stacked = jnp.concatenate([level_rows[:low_total], level_rows[blocks:]], axis=1)
    paired = select(source_table, stacked)
    paired = paired.reshape(lower_idx.shape + (2, fields, width))
    arrived = lax.all_to_all(
        lax.all_to_all(paired, "lat", split_axis=0, concat_axis=0, tiled=True),
        "slab",
        split_axis=1,
        concat_axis=1,
        tiled=True,
    )
    picked = select(arrival_table, arrived.reshape(slot_total, 2 * flat_width))
    picked = picked.reshape(row_total, 2, fields, width)
    scale = weights[:, None, :]
    moved = (1.0 - scale) * picked[:, 0] + scale * picked[:, 1]
    tangent_out = jnp.einsum(
        "flk,gkbfc->glbfc",
        inverse,
        lax.all_to_all(
            moved.reshape(field_state.shape), "slab", split_axis=2, concat_axis=1, tiled=True
        ),
        precision=highest,
    )
    back = jnp.einsum("flk,glbfc->gkbfc", inverse, cotangent, precision=highest)
    back = lax.all_to_all(back, "slab", split_axis=1, concat_axis=2, tiled=True)
    back = back.reshape(row_total, fields, width)
    scale = weights[:, None, :]
    pair_back = jnp.concatenate(
        [
            ((1.0 - scale) * back).reshape(row_total, flat_width),
            (scale * back).reshape(row_total, flat_width),
        ],
        axis=1,
    )
    slot_back = select_back(arrival_table, pair_back)
    returned = lax.all_to_all(
        lax.all_to_all(
            slot_back.reshape(lower_idx.shape + (2, fields, width)),
            "lat",
            split_axis=0,
            concat_axis=0,
            tiled=True,
        ),
        "slab",
        split_axis=1,
        concat_axis=1,
        tiled=True,
    )
    both_back = returned.reshape(slot_total, 2 * flat_width)
    gathered = select_back(source_table, both_back)
    lower_part = jnp.pad(gathered[:, :flat_width], ((0, blocks), (0, 0)))
    upper_part = jnp.pad(gathered[:, flat_width:], ((blocks, 0), (0, 0)))
    adjoint = lower_part + upper_part
    return (tangent_out, adjoint.reshape(field_state.shape))


def solution(mesh):
    placed = (
        P("lat", "slab", None, None, None),
        P("lat", None, "slab", None, None),
        P("lat", "slab", None, None),
        P("lat", None, None, None),
        P("lat", "slab", None, None, None),
        P("lat", "slab", None),
    )
    return jax.shard_map(
        body,
        mesh=mesh,
        in_specs=placed,
        out_specs=(P("lat", None, "slab", None, None), P("lat", "slab", None, None, None)),
        check_vma=False,
    )
```

profile of v0, /device:TPU:1, one launch (start us, length us, event | category | flops | bytes accessed | tf_op | source)
XLA Modules:
  0.0 485.2 jit_solution(521016948758177503)
XLA Ops:
  6.6 8.7 %all-to-all-start.3 = ((f32[1,128,4,5,128]{4,2,3,0,1:T(4,128)}), f32[1,128,4,5,128]{4,2,3,0,1:T(4,128)S(1)}, u32[]{:S(2)}, u32[]{:S(2)}) async-start(f32[1,128,4,5,128]{4,2,3,0,1:T(4,128)} %copy.90), calls=%async_computation.3 | async-start | bytes 2621440 | tf_op jit(solution)/shard_map/all_to_all | solution.py:66
  23.0 6.3 %fusion.8 = f32[1024,1280]{1,0:T(8,128)} fusion(f32[384,640]{0,1:T(8,128)S(1)} %get-tuple-element.20, f32[384,640]{0,1:T(8,128)S(1)} %get-tuple-element.21, s32[1024]{0:T(1024)S(1)} %eq.34), kind=kOutput, calls=%fused_computation.8 | convolution fusion | flops 6040682496 | bytes 7213056 | tf_op jit(solution)/shard_map/dot_general | solution.py:8
  29.3 7.7 %reshape.82 = f32[8,32,4,2,5,128]{5,4,3,2,1,0:T(8,128)} reshape(f32[1024,1280]{1,0:T(8,128)} %fusion.8) | data formatting | bytes 10485760 | tf_op jit(solution)/shard_map/reshape | solution.py:45
  36.9 8.8 %copy.78 = f32[8,32,4,2,5,128]{5,1,4,3,2,0:T(8,128)} copy(f32[8,32,4,2,5,128]{5,4,3,2,1,0:T(8,128)} %reshape.82) | data formatting | bytes 10485760 | tf_op jit(solution)/shard_map/reshape | solution.py:45
  45.7 8.8 %all-to-all-start = ((f32[8,32,4,2,5,128]{5,1,4,3,2,0:T(8,128)}), f32[8,32,4,2,5,128]{5,1,4,3,2,0:T(8,128)}, u32[]{:S(2)}, u32[]{:S(2)}) async-start(f32[8,32,4,2,5,128]{5,1,4,3,2,0:T(8,128)} %copy.78), calls=%async_computation | async-start | bytes 10485760 | tf_op jit(solution)/shard_map/all_to_all | solution.py:47
  58.4 7.1 %fusion = f32[1024,1280]{1,0:T(8,128)} fusion(f32[512,640]{0,1:T(8,128)S(1)} %get-tuple-element.17, f32[512,640]{0,1:T(8,128)S(1)} %get-tuple-element.16, s32[512]{0:T(512)S(1)} %bitcast.76), kind=kOutput, calls=%fused_computation | convolution fusion | flops 8054767616 | bytes 7866368 | tf_op jit(solution)/shard_map/dot_general | solution.py:14
  65.5 7.6 %reshape.87 = f32[8,32,4,2,5,128]{5,4,3,2,1,0:T(8,128)} reshape(f32[1024,1280]{1,0:T(8,128)} %fusion) | data formatting | bytes 10485760 | tf_op jit(solution)/shard_map/reshape | solution.py:79
  73.1 8.7 %copy.96 = f32[8,32,4,2,5,128]{5,1,4,3,2,0:T(8,128)} copy(f32[8,32,4,2,5,128]{5,4,3,2,1,0:T(8,128)} %reshape.87) | data formatting | bytes 10485760 | tf_op jit(solution)/shard_map/reshape | solution.py:79
  81.9 92.0 %all-to-all-done = f32[8,32,4,2,5,128]{5,1,4,3,2,0:T(8,128)} async-done(((f32[8,32,4,2,5,128]{5,1,4,3,2,0:T(8,128)}), f32[8,32,4,2,5,128]{5,1,4,3,2,0:T(8,128)}, u32[]{:S(2)}, u32[]{:S(2)}) %all-to-all-start) | async-done | bytes 5242912 | tf_op jit(solution)/shard_map/all_to_all | solution.py:47
  178.6 7.9 %copy.79 = f32[8,32,4,2,5,128]{5,0,4,3,2,1:T(8,128)} copy(f32[8,32,4,2,5,128]{5,1,4,3,2,0:T(8,128)} %all-to-all-done) | data formatting | bytes 10485760 | tf_op jit(solution)/shard_map/all_to_all | solution.py:47
  186.4 106.2 %all-to-all-done.4 = f32[8,32,4,2,5,128]{5,1,4,3,2,0:T(8,128)} async-done(((f32[8,32,4,2,5,128]{5,1,4,3,2,0:T(8,128)}), f32[8,32,4,2,5,128]{5,1,4,3,2,0:T(8,128)}, u32[]{:S(2)}, u32[]{:S(2)}) %all-to-all-start.4) | async-done | bytes 5242912 | tf_op jit(solution)/shard_map/all_to_all | solution.py:78
  292.6 12.8 %all-to-all-start.1 = ((f32[8,32,4,2,5,128]{5,0,4,3,2,1:T(8,128)}), f32[8,32,4,2,5,128]{5,0,4,3,2,1:T(8,128)}, u32[]{:S(2)}, u32[]{:S(2)}) async-start(f32[8,32,4,2,5,128]{5,0,4,3,2,1:T(8,128)} %copy.79), calls=%async_computation.1 | async-start | bytes 10485760 | tf_op jit(solution)/shard_map/all_to_all | solution.py:46
  305.4 7.9 %copy.97 = f32[8,32,4,2,5,128]{5,0,4,3,2,1:T(8,128)} copy(f32[8,32,4,2,5,128]{5,1,4,3,2,0:T(8,128)} %all-to-all-done.4) | data formatting | bytes 10485760 | tf_op jit(solution)/shard_map/all_to_all | solution.py:78
  313.3 56.7 %all-to-all-done.1 = f32[8,32,4,2,5,128]{5,0,4,3,2,1:T(8,128)} async-done(((f32[8,32,4,2,5,128]{5,0,4,3,2,1:T(8,128)}), f32[8,32,4,2,5,128]{5,0,4,3,2,1:T(8,128)}, u32[]{:S(2)}, u32[]{:S(2)}) %all-to-all-start.1) | async-done | bytes 5242912 | tf_op jit(solution)/shard_map/all_to_all | solution.py:46
  370.0 9.8 %all-to-all-start.5 = ((f32[8,32,4,2,5,128]{5,0,4,3,2,1:T(8,128)}), f32[8,32,4,2,5,128]{5,0,4,3,2,1:T(8,128)}, u32[]{:S(2)}, u32[]{:S(2)}) async-start(f32[8,32,4,2,5,128]{5,0,4,3,2,1:T(8,128)} %copy.97), calls=%async_computation.5 | async-start | bytes 10485760 | tf_op jit(solution)/shard_map/all_to_all | solution.py:77
  380.2 7.4 %copy.80 = f32[8,32,4,2,5,128]{5,4,3,2,1,0:T(8,128)} copy(f32[8,32,4,2,5,128]{5,0,4,3,2,1:T(8,128)} %all-to-all-done.1) | data formatting | bytes 10485760 | tf_op jit(solution)/shard_map/all_to_all | solution.py:46
  387.6 8.2 %reshape.83 = f32[1024,1280]{1,0:T(8,128)} reshape(f32[8,32,4,2,5,128]{5,4,3,2,1,0:T(8,128)} %copy.80) | data formatting | bytes 10485760 | tf_op jit(solution)/shard_map/reshape | solution.py:53
  395.8 6.0 %copy.81 = f32[1280,1024]{1,0:T(8,128)} copy(f32[1280,1024]{0,1:T(8,128)} %bitcast.62) | data formatting | bytes 10485760 | tf_op jit(solution)/shard_map/dot_general | solution.py:8
  401.7 7.7 %fusion.6 = f32[512,2,5,128]{3,0,2,1:T(8,128)S(1)} fusion(f32[2,5,128,1024]{3,2,1,0:T(8,128)} %bitcast.64, s32[512]{0:T(512)S(1)} %bitcast.77), kind=kOutput, calls=%fused_computation.7 | convolution fusion | flops 8053587968 | bytes 7866368 | tf_op jit(solution)/shard_map/dot_general | solution.py:8
  412.6 31.8 %all-to-all-done.5 = f32[8,32,4,2,5,128]{5,0,4,3,2,1:T(8,128)} async-done(((f32[8,32,4,2,5,128]{5,0,4,3,2,1:T(8,128)}), f32[8,32,4,2,5,128]{5,0,4,3,2,1:T(8,128)}, u32[]{:S(2)}, u32[]{:S(2)}) %all-to-all-start.5) | async-done | bytes 5242912 | tf_op jit(solution)/shard_map/all_to_all | solution.py:77
  444.4 8.4 %all-to-all-start.2 = ((f32[1,4,128,5,128]{4,1,3,0,2:T(4,128)}), f32[1,4,128,5,128]{4,1,3,0,2:T(4,128)}, u32[]{:S(2)}, u32[]{:S(2)}) async-start(f32[1,4,128,5,128]{4,1,3,0,2:T(4,128)} %fusion.15), calls=%async_computation.2 | async-start | bytes 2621440 | tf_op jit(solution)/shard_map/all_to_all | solution.py:60
  452.8 7.4 %copy.98 = f32[8,32,4,2,5,128]{5,4,3,2,1,0:T(8,128)} copy(f32[8,32,4,2,5,128]{5,0,4,3,2,1:T(8,128)} %all-to-all-done.5) | data formatting | bytes 10485760 | tf_op jit(solution)/shard_map/all_to_all | solution.py:77
  460.2 8.2 %reshape.88 = f32[1024,1280]{1,0:T(8,128)} reshape(f32[8,32,4,2,5,128]{5,4,3,2,1,0:T(8,128)} %copy.98) | data formatting | bytes 10485760 | tf_op jit(solution)/shard_map/reshape | solution.py:90
  468.4 6.5 %fusion.12 = f32[384,1280]{1,0:T(8,128)S(1)} fusion(f32[1024,1280]{1,0:T(8,128)} %reshape.88, s32[1024]{0:T(1024)S(1)} %eq.34), kind=kOutput, calls=%fused_computation.13 | convolution fusion | flops 6040190976 | bytes 7213056 | tf_op jit(solution)/shard_map/dot_general | solution.py:14
  (41 shorter events, 35.6 us)
Async XLA Ops:
  0.6 1.0 copy-start
  6.6 8.7 %copy-start.3 = (s32[1,1,8,32,4]{3,4,2,1,0:T(4,128)S(1)}, s32[1,1,8,32,4]{3,4,2,1,0:T(4,128)}, u32[]{:S(2)}) copy-start(s32[1,1,8,32,4]{3,4,2,1,0:T(4,128)} %param.10) | copy-start | bytes 12292
  6.6 9.0 %copy-start.1 = (f32[1,4,128,5,128]{4,2,3,1,0:T(8,128)S(1)}, f32[1,4,128,5,128]{4,2,3,1,0:T(8,128)}, u32[]{:S(2)}) copy-start(f32[1,4,128,5,128]{4,2,3,1,0:T(8,128)} %param.6) | copy-start | bytes 3932164
  6.6 39.1 %all-to-all-start.3 = ((f32[1,128,4,5,128]{4,2,3,0,1:T(4,128)}), f32[1,128,4,5,128]{4,2,3,0,1:T(4,128)S(1)}, u32[]{:S(2)}, u32[]{:S(2)}) async-start(f32[1,128,4,5,128]{4,2,3,0,1:T(4,128)} %copy.90), calls=%async_computation.3 | async-start | bytes 2621440 | tf_op jit(solution)/shard_map/all_to_all | solution.py:66
  45.7 8.8 %copy-start.2 = (f32[1,4,128,128]{3,2,1,0:T(8,128)S(1)}, f32[1,4,128,128]{3,2,1,0:T(8,128)}, u32[]{:S(2)}) copy-start(f32[1,4,128,128]{3,2,1,0:T(8,128)} %param.8) | copy-start | bytes 786436
  45.7 128.2 %all-to-all-start = ((f32[8,32,4,2,5,128]{5,1,4,3,2,0:T(8,128)}), f32[8,32,4,2,5,128]{5,1,4,3,2,0:T(8,128)}, u32[]{:S(2)}, u32[]{:S(2)}) async-start(f32[8,32,4,2,5,128]{5,1,4,3,2,0:T(8,128)} %copy.78), calls=%async_computation | async-start | bytes 10485760 | tf_op jit(solution)/shard_map/all_to_all | solution.py:47
  57.1 1.3 copy-start.4
  173.9 118.7 %all-to-all-start.4 = ((f32[8,32,4,2,5,128]{5,1,4,3,2,0:T(8,128)}), f32[8,32,4,2,5,128]{5,1,4,3,2,0:T(8,128)}, u32[]{:S(2)}, u32[]{:S(2)}) async-start(f32[8,32,4,2,5,128]{5,1,4,3,2,0:T(8,128)} %copy.96), calls=%async_computation.4 | async-start | bytes 10485760 | tf_op jit(solution)/shard_map/all_to_all | solution.py:78
  292.6 77.3 %all-to-all-start.1 = ((f32[8,32,4,2,5,128]{5,0,4,3,2,1:T(8,128)}), f32[8,32,4,2,5,128]{5,0,4,3,2,1:T(8,128)}, u32[]{:S(2)}, u32[]{:S(2)}) async-start(f32[8,32,4,2,5,128]{5,0,4,3,2,1:T(8,128)} %copy.79), calls=%async_computation.1 | async-start | bytes 10485760 | tf_op jit(solution)/shard_map/all_to_all | solution.py:46
  370.0 74.4 %all-to-all-start.5 = ((f32[8,32,4,2,5,128]{5,0,4,3,2,1:T(8,128)}), f32[8,32,4,2,5,128]{5,0,4,3,2,1:T(8,128)}, u32[]{:S(2)}, u32[]{:S(2)}) async-start(f32[8,32,4,2,5,128]{5,0,4,3,2,1:T(8,128)} %copy.97), calls=%async_computation.5 | async-start | bytes 10485760 | tf_op jit(solution)/shard_map/all_to_all | solution.py:77
  444.4 34.5 %all-to-all-start.2 = ((f32[1,4,128,5,128]{4,1,3,0,2:T(4,128)}), f32[1,4,128,5,128]{4,1,3,0,2:T(4,128)}, u32[]{:S(2)}, u32[]{:S(2)}) async-start(f32[1,4,128,5,128]{4,1,3,0,2:T(4,128)} %fusion.15), calls=%async_computation.2 | async-start | bytes 2621440 | tf_op jit(solution)/shard_map/all_to_all | solution.py:60
where the time goes:
time: 494 us; the launch traced here: 485 us
  waiting for transfers between devices  287 us (58%)
  local copies, waits for them, and re-layouts  105 us (21%)
  starting transfers between devices  53.2 us (11%)
  matrix products  33.3 us (7%)
  other arithmetic  6.18 us (1%)
    all_to_all x1, waiting for transfers between devices, body(): lax.all_to_all(slot_back.reshape(lower_idx.shape + (2, fields, width)), '...  106 us
    all_to_all x1, waiting for transfers between devices, body(): lax.all_to_all(paired, 'lat', split_axis=0, concat_axis=0, tiled=True)  92 us
    all_to_all x1, waiting for transfers between devices, body(): lax.all_to_all(lax.all_to_all(paired, 'lat', split_axis=0, concat_axis=0,...  56.7 us
    all_to_all x1, waiting for transfers between devices, body(): lax.all_to_all(lax.all_to_all(slot_back.reshape(lower_idx.shape + (2, fie...  31.8 us
    reshape x2, local copies, waits for them, and re-layouts, body(): paired = paired.reshape(lower_idx.shape + (2, fields, width))  16.4 us
    reshape x2, local copies, waits for them, and re-layouts, body(): slot_back.reshape(lower_idx.shape + (2, fields, width))  16.4 us
    dot_general x2, matrix products, select(): jnp.dot(table, values, precision=lax.Precision.HIGHEST, preferred_element...  14 us
    dot_general x2, matrix products, select_back(): lax.dot_general(table, values, (((0,), (0,)), ((), ())), precision=lax.Pr...  13.6 us
  transfers between devices with their start and end apart: 6, of which 4 were waited for; matrix products, arithmetic and copies ran while one was open for 27% of the time, Pallas kernels for 0%

commit v1 on v0

v1 whole, which is shorter than its diff:
```python
import functools

import jax
import jax.numpy as jnp
from jax import lax
from jax.experimental import pallas as pl
from jax.experimental.pallas import tpu as pltpu
from jax.sharding import PartitionSpec as P

MESH = pl.DeviceIdType.MESH
VMEM_LIMIT = 56 << 20
F32 = jnp.float32
BF16 = jnp.bfloat16


def two_part_dot(table, values):
    high = values.astype(BF16)
    low = (values - high.astype(F32)).astype(BF16)
    return jnp.dot(table, high, preferred_element_type=F32) + jnp.dot(
        table, low, preferred_element_type=F32
    )


def one_hot(shape, ids, axis):
    return (lax.broadcasted_iota(jnp.int32, shape, axis) == ids).astype(F32).astype(BF16)


def columns_of(ref, f, fields, per, levels):
    parts = [ref[pl.ds(f * per + b, levels, stride=fields * per), :] for b in range(per)]
    return jnp.concatenate(parts, axis=1)


def start_kernel(fields, per, levels, slots, weights, cot, inverse, weight_out, back_out):
    table = one_hot((weight_out.shape[0], slots.shape[1]), slots[...], 0)
    weight_out[...] = two_part_dot(table, weights[...])
    for f in range(fields):
        out = lax.dot_general(
            inverse[f],
            columns_of(cot, f, fields, per, levels),
            (((0,), (0,)), ((), ())),
            precision=lax.Precision.HIGHEST,
            preferred_element_type=F32,
        )
        for b in range(per):
            back_out[pl.ds(f * per + b, levels, stride=fields * per), :] = out[:, b * 128 : (b + 1) * 128]


def spread_kernel(fields, slots, back, out):
    rows = slots.shape[1]
    table = one_hot((out.shape[1], rows), slots[...], 0)
    for f in range(fields):
        out[f] = two_part_dot(table, back[:, f].reshape(rows, 128))


def gather_kernel(fields, lower, weights, state, out):
    low_rows = 3 * 128
    table = one_hot((out.shape[1], low_rows), lower[...], 1)
    upper_part = weights[...]
    for f in range(fields):
        both = jnp.concatenate(
            [state[0:3, f].reshape(low_rows, 128), state[1:4, f].reshape(low_rows, 128)], axis=1
        )
        picked = two_part_dot(table, both)
        out[f] = (1.0 - upper_part) * picked[:, :128] + upper_part * picked[:, 128:]


def arrive_kernel(fields, slots, arrived, out):
    rows = slots.shape[0]
    table = one_hot((rows, arrived.shape[1]), slots[...], 1)
    for f in range(fields):
        out[:, f] = two_part_dot(table, arrived[f]).reshape(4, 128, 128)


def finish_kernel(fields, per, levels, moved, inverse, out):
    for f in range(fields):
        res = jnp.dot(
            inverse[f],
            columns_of(moved, f, fields, per, levels),
            precision=lax.Precision.HIGHEST,
            preferred_element_type=F32,
        )
        for b in range(per):
            out[pl.ds(f * per + b, levels, stride=fields * per), :] = res[:, b * 128 : (b + 1) * 128]


def scatter_kernel(fields, lower, weights, back, out):
    low_rows = 3 * 128
    table = one_hot((low_rows, lower.shape[1]), lower[...], 0)
    upper_part = weights[...]
    for f in range(fields):
        row = back[f]
        both = two_part_dot(
            table, jnp.concatenate([(1.0 - upper_part) * row, upper_part * row], axis=1)
        )
        low, high = both[:, :128].reshape(3, 128, 128), both[:, 128:].reshape(3, 128, 128)
        out[0, f] = low[0]
        out[1, f] = low[1] + high[0]
        out[2, f] = low[2] + high[1]
        out[3, f] = high[2]


def local(body, shapes, *args):
    return pl.pallas_call(
        body,
        out_shape=shapes,
        in_specs=[pl.BlockSpec(memory_space=pltpu.VMEM)] * len(args),
        out_specs=jax.tree.map(lambda _: pl.BlockSpec(memory_space=pltpu.VMEM), shapes),
        compiler_params=pltpu.CompilerParams(vmem_limit_bytes=VMEM_LIMIT),
    )(*args)


def shape(*dims):
    return jax.ShapeDtypeStruct(dims, F32)


def greet(g, s, n_lat, n_slab, lat, slab):
    bar = pltpu.get_barrier_semaphore()
    count = 0
    if lat:
        for k in range(1, n_lat):
            pl.semaphore_signal(bar, inc=1, device_id=((g + k) % n_lat, s), device_id_type=MESH)
        count += n_lat - 1
    if slab:

        def one(k, carry):
            pl.semaphore_signal(bar, inc=1, device_id=(g, (s + k) % n_slab), device_id_type=MESH)
            return carry

        lax.fori_loop(1, n_slab, one, 0)
        count += n_slab - 1
    pl.semaphore_wait(bar, count)


def slab_sends(g, s, n_slab, source, target, send, recv):
    pltpu.make_async_copy(source(s), target(s), recv).start()

    def one(k, carry):
        peer = (s + k) % n_slab
        pltpu.make_async_remote_copy(
            source(peer), target(s), send, recv, device_id=(g, peer), device_id_type=MESH
        ).start()
        return carry

    lax.fori_loop(1, n_slab, one, 0)


def lat_sends(g, s, n_lat, source, target, send, recv):
    pltpu.make_async_copy(source(g), target(g), recv).start()
    for k in (4, 1, 7, 2, 6, 3, 5):
        peer = (g + k) % n_lat
        pltpu.make_async_remote_copy(
            source(peer), target(g), send, recv, device_id=(peer, s), device_id_type=MESH
        ).start()


def wait_all(ref, sem):
    pltpu.make_async_copy(ref, ref, sem).wait()


def begin_comm(x, back, o, rows, xb, xs, xr, zs, zr, bs, br):
    g, s = lax.axis_index("lat"), lax.axis_index("slab")
    n_slab, n_lat = x.shape[0], x.shape[1]
    greet(g, s, n_lat, n_slab, True, True)
    slab_sends(g, s, n_slab, lambda p: x.at[p], lambda p: xb.at[p], xs, xr)
    slab_sends(g, s, n_slab, lambda p: back.at[p], lambda p: rows.at[:, :, p], bs, br)
    wait_all(xb, xr)
    lat_sends(g, s, n_lat, lambda p: xb.at[:, p], lambda p: o.at[p], zs, zr)
    wait_all(o, zr)
    wait_all(rows, br)
    wait_all(xb.at[: n_slab - 1], xs)
    wait_all(o.at[: n_lat - 1], zs)
    wait_all(back.at[: n_slab - 1], bs)


def forward_comm(x, o, zb, zs, zr, xs, xr):
    g, s = lax.axis_index("lat"), lax.axis_index("slab")
    fields, n_lat, n_slab = x.shape[:3]
    greet(g, s, n_lat, n_slab, True, True)
    for f in range(fields):
        lat_sends(g, s, n_lat, lambda p: x.at[f, p], lambda p: zb.at[f, p], zs.at[f], zr.at[f])
    for f in range(fields):
        wait_all(zb.at[f], zr.at[f])
        slab_sends(g, s, n_slab, lambda p: zb.at[f, :, p], lambda p: o.at[f, p], xs.at[f], xr.at[f])
    for f in range(fields):
        wait_all(o.at[f], xr.at[f])
        wait_all(x.at[f, : n_lat - 1], zs.at[f])
        wait_all(o.at[f, : n_slab - 1], xs.at[f])


def adjoint_comm(x, moved, o, levels, xb, xs, xr, zs, zr, ms, mr):
    g, s = lax.axis_index("lat"), lax.axis_index("slab")
    fields, n_slab, n_lat = x.shape[:3]
    greet(g, s, n_lat, n_slab, True, True)
    for f in range(fields):
        slab_sends(g, s, n_slab, lambda p: x.at[f, p], lambda p: xb.at[f, p], xs.at[f], xr.at[f])
    slab_sends(g, s, n_slab, lambda p: moved.at[:, :, p], lambda p: levels.at[p], ms, mr)
    for f in range(fields):
        wait_all(xb.at[f], xr.at[f])
        lat_sends(g, s, n_lat, lambda p: xb.at[f, :, p], lambda p: o.at[f, p], zs.at[f], zr.at[f])
    for f in range(fields):
        wait_all(o.at[f], zr.at[f])
        wait_all(o.at[f, : n_lat - 1], zs.at[f])
        wait_all(x.at[f, : n_slab - 1], xs.at[f])
    wait_all(levels, mr)
    wait_all(levels.at[: n_slab - 1], ms)


def comm(body, cid, shapes, scratch, *args):
    return pl.pallas_call(
        body,
        out_shape=shapes,
        in_specs=[pl.BlockSpec(memory_space=pl.ANY)] * len(args),
        out_specs=jax.tree.map(lambda _: pl.BlockSpec(memory_space=pl.ANY), shapes),
        scratch_shapes=scratch,
        compiler_params=pltpu.CompilerParams(
            vmem_limit_bytes=VMEM_LIMIT, collective_id=cid, has_side_effects=True
        ),
    )(*args)


def body(field_state, cotangent, vertical_weight, diffusion_inverse, source_row, dest_slot):
    _, here, blocks, fields, width = field_state.shape
    levels, per = cotangent.shape[1], cotangent.shape[2]
    n_lat, n_slab, cap = source_row.shape[2:]
    rows = here * blocks
    slot_total = n_lat * n_slab * cap
    dma = pltpu.SemaphoreType.DMA

    state = field_state.transpose(0, 1, 3, 2, 4).reshape(here, fields, blocks, width)
    cot = cotangent.transpose(0, 1, 3, 2, 4).reshape(levels * fields * per, width)
    weights = vertical_weight.reshape(rows, width)
    inverse = diffusion_inverse[0]
    lower = source_row.reshape(slot_total)
    slots = dest_slot.reshape(rows)
    sender, slot = slots // cap, slots % cap
    slots = ((sender % n_slab) * n_lat + sender // n_slab) * cap + slot
    slots_row, slots_col = slots.reshape(1, rows), slots.reshape(rows, 1)
    lower_row, lower_col = lower.reshape(1, slot_total), lower.reshape(slot_total, 1)

    weight_slots, back = local(
        functools.partial(start_kernel, fields, per, levels),
        (shape(slot_total, width), shape(levels * fields * per, width)),
        slots_row, weights, cot, inverse,
    )
    weight_own, back_rows = comm(
        begin_comm, 0,
        (shape(n_lat, n_slab, cap, width), shape(here, fields, n_slab, per, width)),
        [pltpu.VMEM((n_slab, n_lat, cap, width), F32)] + [dma] * 6,
        weight_slots.reshape(n_slab, n_lat, cap, width),
        back.reshape(n_slab, here, fields, per, width),
    )
    weight_own = weight_own.reshape(slot_total, width)
    sent = local(
        functools.partial(gather_kernel, fields), shape(fields, slot_total, width), lower_col, weight_own, state
    )
    arrived = comm(
        forward_comm, 1,
        shape(fields, n_slab, n_lat, cap, width),
        [pltpu.VMEM((fields, n_lat, n_slab, cap, width), F32)] + [dma((fields,))] * 4,
        sent.reshape(fields, n_lat, n_slab, cap, width),
    )
    moved = local(
        functools.partial(arrive_kernel, fields),
        shape(here, fields, blocks, width),
        slots_col, arrived.reshape(fields, slot_total, width),
    )
    spread = local(
        functools.partial(spread_kernel, fields),
        shape(fields, slot_total, width),
        slots_row, back_rows.reshape(here, fields, blocks, width),
    )
    returned, by_level = comm(
        adjoint_comm, 2,
        (shape(fields, n_lat, n_slab, cap, width), shape(n_slab, here, fields, per, width)),
        [pltpu.VMEM((fields, n_slab, n_lat, cap, width), F32)] + [dma((fields,))] * 4 + [dma] * 2,
        spread.reshape(fields, n_slab, n_lat, cap, width),
        moved.reshape(here, fields, n_slab, per, width),
    )
    tangent = local(
        functools.partial(finish_kernel, fields, per, levels),
        shape(levels * fields * per, width),
        by_level.reshape(levels * fields * per, width), inverse,
    )
    adjoint = local(
        functools.partial(scatter_kernel, fields),
        shape(here, fields, blocks, width),
        lower_row, weight_own, returned.reshape(fields, slot_total, width),
    )
    tangent = tangent.reshape(1, levels, fields, per, width).transpose(0, 1, 3, 2, 4)
    adjoint = adjoint.reshape(1, here, fields, blocks, width).transpose(0, 1, 3, 2, 4)
    return tangent, adjoint


def solution(mesh):
    placed = (
        P("lat", "slab", None, None, None),
        P("lat", None, "slab", None, None),
        P("lat", "slab", None, None),
        P("lat", None, None, None),
        P("lat", "slab", None, None, None),
        P("lat", "slab", None),
    )
    return jax.shard_map(
        body,
        mesh=mesh,
        in_specs=placed,
        out_specs=(P("lat", None, "slab", None, None), P("lat", "slab", None, None, None)),
        check_vma=False,
    )
```

time: 494 us -> 231 us (0.47); the launches traced: 485 us -> 231 us
  waiting for transfers between devices: 287 us -> 0 us
  Pallas kernels: 0 us -> 226 us
  local copies, waits for them, and re-layouts: 105 us -> 1.97 us
  starting transfers between devices: 53.2 us -> 0 us
  matrix products: 33.3 us -> 0 us
    all_to_all x6 -> x0, waiting for transfers between devices: 287 us -> none  [the longest x1 106 us: body(): lax.all_to_all(slot_back.reshape(lower_idx.shape + (2, fields, width)), '...]
    pallas_call x0 -> x9, Pallas kernels: none -> 226 us  [the longest x3 195 us: comm(): pl.pallas_call(body, out_shape=shapes, in_specs=[pl.BlockSpec(memory_spac...]
    all_to_all x6 -> x0, starting transfers between devices: 53.2 us -> none  [the longest x1 12.8 us: body(): lax.all_to_all(lax.all_to_all(paired, 'lat', split_axis=0, concat_axis=0,...]
    reshape x8 -> x1, local copies, waits for them, and re-layouts: 51 us -> 0.14 us  [body(): slots = dest_slot.reshape(rows)]
    all_to_all x8 -> x0, local copies, waits for them, and re-layouts: 33.8 us -> none  [the longest x1 7.89 us: body(): lax.all_to_all(slot_back.reshape(lower_idx.shape + (2, fields, width)), '...]
    dot_general x6 -> x0, matrix products: 33.3 us -> none  [the longest x2 14 us: select(): jnp.dot(table, values, precision=lax.Precision.HIGHEST, preferred_element...]
    slice x6 -> x0, local copies, waits for them, and re-layouts: 7.69 us -> none  [the longest x2 3.93 us: body(): level_rows[blocks:]]
    dot_general x1 -> x0, local copies, waits for them, and re-layouts: 5.96 us -> none  [select(): jnp.dot(table, values, precision=lax.Precision.HIGHEST, preferred_element...]
  transfers between devices with their start and end apart: 6 -> 0, of which waited for: 4 -> 0; matrix products, arithmetic and copies ran while one was open for 27% -> 0% of each run, Pallas kernels for 0% -> 0%
where the time goes in v1:
time: 231 us
  Pallas kernels  226 us (98%)
  other arithmetic  2.5 us (1%)
    pallas_call x3, Pallas kernels, comm(): pl.pallas_call(body, out_shape=shapes, in_specs=[pl.BlockSpec(memory_spac...  195 us
    pallas_call x6, Pallas kernels, local(): pl.pallas_call(body, out_shape=shapes, in_specs=[pl.BlockSpec(memory_spac...  30.8 us

profile of v1, /device:TPU:1, one launch (start us, length us, event | category | flops | bytes accessed | tf_op | source)
XLA Modules:
  0.0 230.8 jit_solution(9759451805686733211)
XLA Ops:
  0.6 1.3 fusion.10.slots
  1.9 4.3 %shard_map.77 = (f32[1024,128]{1,0:T(8,128)}, f32[2560,128]{1,0:T(8,128)}) custom-call(s32[1,512]{1,0:T(1,128)} %fusion.10.slots, f32[512,128]{1,0:T(8,128)} %bitcast.59, f32[2560,128]{1,0:T(8,128)} %bitcast.52, f32[5,128,128]{2,1,0:T(8,128)} %bitcast.56), custom_call_target="tpu_custom_call" | custom-call | tf_op jit(solution)/shard_map/pallas_call | solution.py:103
  6.2 0.0 copy-start
  6.2 36.6 %shard_map.78 = (f32[8,32,4,128]{3,2,1,0:T(4,128)}, f32[4,5,32,4,128]{4,3,2,1,0:T(4,128)}) custom-call(f32[32,8,4,128]{3,2,1,0:T(4,128)} %bitcast.58, f32[32,4,5,4,128]{4,3,2,1,0:T(4,128)} %bitcast.51), custom_call_target="tpu_custom_call" | custom-call | tf_op jit(solution)/shard_map/pallas_call | solution.py:209
  42.8 0.0 copy-done
  42.8 0.1 copy.14
  43.0 1.0 reshape_reshape.8.lower
  43.9 6.1 %shard_map.80 = f32[5,1024,128]{2,1,0:T(8,128)} custom-call(s32[1024,1]{1,0:T(8,128)} %reshape_reshape.8.lower, f32[1024,128]{1,0:T(8,128)} %bitcast.47, f32[4,5,128,128]{3,2,1,0:T(8,128)} %bitcast.55), custom_call_target="tpu_custom_call" | custom-call | tf_op jit(solution)/shard_map/pallas_call | solution.py:103
  50.0 0.0 copy-start.1
  50.0 82.2 %shard_map.81 = f32[5,32,8,4,128]{4,3,2,1,0:T(4,128)} custom-call(f32[5,8,32,4,128]{4,3,2,1,0:T(4,128)} %bitcast.44), custom_call_target="tpu_custom_call" | custom-call | tf_op jit(solution)/shard_map/pallas_call | solution.py:209
  132.2 0.0 copy-done.1
  132.2 0.1 copy.10
  132.4 1.2 fusion.3.slots
  133.6 5.9 %shard_map.82 = f32[4,5,128,128]{3,2,1,0:T(8,128)} custom-call(s32[512,1]{1,0:T(8,128)} %fusion.3.slots, f32[5,1024,128]{2,1,0:T(8,128)} %bitcast.43), custom_call_target="tpu_custom_call" | custom-call | tf_op jit(solution)/shard_map/pallas_call | solution.py:103
  139.4 5.7 %shard_map.79 = f32[5,1024,128]{2,1,0:T(8,128)} custom-call(s32[1,512]{1,0:T(1,128)} %fusion.10.slots, f32[4,5,128,128]{3,2,1,0:T(8,128)} %bitcast.49), custom_call_target="tpu_custom_call" | custom-call | tf_op jit(solution)/shard_map/pallas_call | solution.py:103
  145.1 76.1 %shard_map.83 = (f32[5,8,32,4,128]{4,3,2,1,0:T(4,128)}, f32[32,4,5,4,128]{4,3,2,1,0:T(4,128)}) custom-call(f32[5,32,8,4,128]{4,3,2,1,0:T(4,128)} %bitcast.42, f32[4,5,32,4,128]{4,3,2,1,0:T(4,128)} %bitcast.45), custom_call_target="tpu_custom_call" | custom-call | tf_op jit(solution)/shard_map/pallas_call | solution.py:209
  221.2 0.7 reshape_reshape.7.lower
  221.9 5.2 %shard_map.85 = f32[4,5,128,128]{3,2,1,0:T(8,128)} custom-call(s32[1,1024]{1,0:T(1,128)} %reshape_reshape.7.lower, f32[1024,128]{1,0:T(8,128)} %bitcast.48, f32[5,1024,128]{2,1,0:T(8,128)} %bitcast.46), custom_call_target="tpu_custom_call" | custom-call | tf_op jit(solution)/shard_map/pallas_call | solution.py:103
  227.2 3.6 %shard_map.84 = f32[2560,128]{1,0:T(8,128)} custom-call(f32[2560,128]{1,0:T(8,128)} %bitcast.53, f32[5,128,128]{2,1,0:T(8,128)} %bitcast.57), custom_call_target="tpu_custom_call" | custom-call | tf_op jit(solution)/shard_map/pallas_call | solution.py:103
Async XLA Ops:
  6.2 36.6 %copy-start = (s32[1,1,8,32,4]{3,4,2,1,0:T(4,128)S(1)}, s32[1,1,8,32,4]{3,4,2,1,0:T(4,128)}, u32[]{:S(2)}) copy-start(s32[1,1,8,32,4]{3,4,2,1,0:T(4,128)} %param.10) | copy-start | bytes 12292
  50.0 82.2 %copy-start.1 = (s32[1,1,512]{2,1,0:T(1,128)S(1)}, s32[1,1,512]{2,1,0:T(1,128)}, u32[]{:S(2)}) copy-start(s32[1,1,512]{2,1,0:T(1,128)} %param.11) | copy-start | bytes 6148

commit v2 on v0

v2 whole, which is shorter than its diff:
```python
import functools

import jax
import jax.numpy as jnp
from jax import lax
from jax.experimental import pallas as pl
from jax.experimental.pallas import tpu as pltpu
from jax.sharding import PartitionSpec as P

MESH = pl.DeviceIdType.MESH
VMEM_LIMIT = 60 << 20
F32 = jnp.float32
BF16 = jnp.bfloat16


def split(values):
    high = values.astype(BF16)
    return high, (values - high.astype(F32)).astype(BF16)


def pick(table, values):
    width = values.shape[1]
    out = jnp.dot(table, jnp.concatenate(split(values), axis=1), preferred_element_type=F32)
    return out[:, :width] + out[:, width:]


def one_hot(shape, ids, axis):
    return (lax.broadcasted_iota(jnp.int32, shape, axis) == ids).astype(F32).astype(BF16)


def side_by_side(view, first, stride, per, levels):
    parts = [view[pl.ds(first + b, levels, stride=stride), :] for b in range(per)]
    return jnp.concatenate(parts, axis=1)


def lay_down(view, first, stride, per, levels, values):
    for b in range(per):
        view[pl.ds(first + b, levels, stride=stride), :] = values[:, b * 128 : (b + 1) * 128]


def signal_peers(g, s, n_lat, n_slab):
    bar = pltpu.get_barrier_semaphore()
    for k in range(1, n_lat):
        pl.semaphore_signal(bar, inc=1, device_id=((g + k) % n_lat, s), device_id_type=MESH)

    def one(k, carry):
        pl.semaphore_signal(bar, inc=1, device_id=(g, (s + k) % n_slab), device_id_type=MESH)
        return carry

    lax.fori_loop(1, n_slab, one, 0)


def wait_all(ref, sem):
    pltpu.make_async_copy(ref, ref, sem).wait()


def whole(
    slots_row, slots_col, lower_row, lower_col, weights, inverse, cot, state,
    tangent, adjoint,
    to_slot, from_slot, to_row, from_row,
    wx, wz, wo, bx, bk, fx, fz, fo, ax, ab, ao, mx, mo,
    w_sem, b_send, b_recv, fz_send, fz_recv, fx_send, fx_recv,
    az_send, az_recv, ax_send, ax_recv, m_send, m_recv,
):
    g, s = lax.axis_index("lat"), lax.axis_index("slab")
    fields, n_lat, n_slab, cap = fx.shape[:4]
    here, per = bk.shape[1], bk.shape[3]
    levels = n_slab * here
    blocks = n_slab * per
    slot_total = n_lat * n_slab * cap
    rows = here * blocks
    low_rows = rows - blocks

    def slab_sends(source, target, send, recv):
        pltpu.make_async_copy(source(s), target(s), recv).start()

        def one(k, carry):
            peer = (s + k) % n_slab
            pltpu.make_async_remote_copy(
                source(peer), target(s), send, recv, device_id=(g, peer), device_id_type=MESH
            ).start()
            return carry

        lax.fori_loop(1, n_slab, one, 0)

    def lat_sends(source, target, send, recv):
        pltpu.make_async_copy(source(g), target(g), recv).start()
        for k in (4, 1, 7, 2, 6, 3, 5):
            peer = (g + k) % n_lat
            pltpu.make_async_remote_copy(
                source(peer), target(g), send, recv, device_id=(peer, s), device_id_type=MESH
            ).start()

    def slot_rows(ref):
        return ref.reshape(fields * slot_total, 128)

    def local_rows(ref):
        return ref.reshape(fields * rows, 128)

    def at_field(f, count):
        return pl.ds(f * count, count)

    signal_peers(g, s, n_lat, n_slab)
    to_slot[...] = one_hot((slot_total, rows), slots_row[...], 0)
    wx.reshape(slot_total, 128)[...] = pick(to_slot[...], weights[...])
    pl.semaphore_wait(pltpu.get_barrier_semaphore(), n_lat + n_slab - 2)
    lat_sends(lambda p: wx.at[p], lambda p: wz.at[p], w_sem.at[0], w_sem.at[1])

    def backward(f):
        out = lax.dot_general(
            inverse[f],
            side_by_side(cot, f * per, fields * per, per, levels),
            (((0,), (0,)), ((), ())),
            precision=lax.Precision.HIGHEST,
            preferred_element_type=F32,
        )
        lay_down(local_rows(bx), f * rows, per, per, levels, out)
        slab_sends(lambda p: bx.at[f, p], lambda p: bk.at[f, :, p], b_send.at[f], b_recv.at[f])

    def spread(f):
        wait_all(bk.at[f], b_recv.at[f])
        slot_rows(ax)[at_field(f, slot_total), :] = pick(
            to_slot[...], local_rows(bk)[at_field(f, rows), :]
        )

    def gather(f):
        both = jnp.concatenate(
            [
                state[0 : here - 1, f].reshape(low_rows, 128),
                state[1:here, f].reshape(low_rows, 128),
            ],
            axis=1,
        )
        picked = pick(from_row[...], both)
        part = wo.reshape(slot_total, 128)[...]
        slot_rows(fx)[at_field(f, slot_total), :] = (1.0 - part) * picked[:, :128] + part * picked[:, 128:]
        lat_sends(lambda p: fx.at[f, p], lambda p: fz.at[f, p], fz_send.at[f], fz_recv.at[f])

    def pass_on(f):
        wait_all(fz.at[f], fz_recv.at[f])
        slab_sends(lambda p: fz.at[f, :, p], lambda p: fo.at[f, :, p], fx_send.at[f], fx_recv.at[f])

    def arrive(f):
        wait_all(fo.at[f], fx_recv.at[f])
        local_rows(mx)[at_field(f, rows), :] = pick(
            from_slot[...], slot_rows(fo)[at_field(f, slot_total), :]
        )
        slab_sends(lambda p: mx.at[f, :, p], lambda p: mo.at[f, p], m_send.at[f], m_recv.at[f])

    def finish(f):
        wait_all(mo.at[f], m_recv.at[f])
        out = jnp.dot(
            inverse[f],
            side_by_side(local_rows(mo), f * rows, per, per, levels),
            precision=lax.Precision.HIGHEST,
            preferred_element_type=F32,
        )
        lay_down(tangent, f * per, fields * per, per, levels, out)

    def adjoint_slab(f):
        slab_sends(lambda p: ax.at[f, :, p], lambda p: ab.at[f, :, p], ax_send.at[f], ax_recv.at[f])

    def adjoint_lat(f):
        wait_all(ab.at[f], ax_recv.at[f])
        lat_sends(lambda p: ab.at[f, p], lambda p: ao.at[f, p], az_send.at[f], az_recv.at[f])

    def scatter(f, sem):
        wait_all(ao.at[f], sem)
        row = slot_rows(ao)[at_field(f, slot_total), :]
        part = wo.reshape(slot_total, 128)[...]
        both = pick(to_row[...], jnp.concatenate([(1.0 - part) * row, part * row], axis=1))
        low = both[:, :128].reshape(here - 1, blocks, 128)
        high = both[:, 128:].reshape(here - 1, blocks, 128)
        adjoint[0, f] = low[0]
        for l in range(1, here - 1):
            adjoint[l, f] = low[l] + high[l - 1]
        adjoint[here - 1, f] = high[here - 2]

    for f in range(fields):
        backward(f)
    from_row[...] = one_hot((slot_total, low_rows), lower_col[...], 1)
    spread(0)
    lat_sends(lambda p: ax.at[0, p], lambda p: ab.at[0, p], az_send.at[0], az_recv.at[0])
    wait_all(wz, w_sem.at[1])
    slab_sends(lambda p: wz.at[:, p], lambda p: wo.at[:, p], w_sem.at[2], w_sem.at[3])
    spread(1)
    wait_all(wo, w_sem.at[3])
    for f in range(fields):
        gather(f)
    wait_all(ab.at[0], az_recv.at[0])
    slab_sends(lambda p: ab.at[0, :, p], lambda p: ao.at[0, :, p], ax_send.at[0], ax_recv.at[0])
    adjoint_slab(1)
    for f in range(2, fields):
        spread(f)
        adjoint_slab(f)
    from_slot[...] = one_hot((rows, slot_total), slots_col[...], 1)
    to_row[...] = one_hot((low_rows, slot_total), lower_row[...], 0)
    for f in range(fields):
        pass_on(f)
        if f == 0:
            scatter(0, ax_recv.at[0])
        if f >= 1:
            adjoint_lat(f)
            arrive(f - 1)
        if f >= 2:
            finish(f - 2)
    arrive(fields - 1)
    finish(fields - 2)
    finish(fields - 1)
    for f in range(1, fields):
        scatter(f, az_recv.at[f])

    wait_all(wz.at[: n_lat - 1], w_sem.at[0])
    wait_all(wo.at[:, : n_slab - 1], w_sem.at[2])
    for f in range(fields):
        wait_all(bx.at[f, : n_slab - 1], b_send.at[f])
        wait_all(fz.at[f, : n_lat - 1], fz_send.at[f])
        wait_all(fo.at[f, :, : n_slab - 1], fx_send.at[f])
        wait_all(mo.at[f, : n_slab - 1], m_send.at[f])
        wait_all(ao.at[f, : n_lat - 1], az_send.at[f])
        wait_all(ab.at[f, :, : n_slab - 1], ax_send.at[f])


def body(field_state, cotangent, vertical_weight, diffusion_inverse, source_row, dest_slot):
    _, here, blocks, fields, width = field_state.shape
    levels, per = cotangent.shape[1], cotangent.shape[2]
    n_lat, n_slab, cap = source_row.shape[2:]
    rows = here * blocks
    slot_total = n_lat * n_slab * cap
    low_rows = rows - blocks
    dma = pltpu.SemaphoreType.DMA

    state = field_state.transpose(0, 1, 3, 2, 4).reshape(here, fields, blocks, width)
    cot = cotangent.transpose(0, 1, 3, 2, 4).reshape(levels * fields * per, width)
    lower = source_row.reshape(slot_total)
    slots = dest_slot.reshape(rows)
    vmem = pl.BlockSpec(memory_space=pltpu.VMEM)
    slot_array = pltpu.VMEM((fields, n_lat, n_slab, cap, width), F32)
    weight_array = pltpu.VMEM((n_lat, n_slab, cap, width), F32)
    by_level = pltpu.VMEM((fields, here, n_slab, per, width), F32)
    by_block = pltpu.VMEM((fields, n_slab, here, per, width), F32)

    tangent, adjoint = pl.pallas_call(
        whole,
        out_shape=(
            jax.ShapeDtypeStruct((levels * fields * per, width), F32),
            jax.ShapeDtypeStruct((here, fields, blocks, width), F32),
        ),
        in_specs=[vmem] * 8,
        out_specs=(vmem, vmem),
        scratch_shapes=[
            pltpu.VMEM((slot_total, rows), BF16),
            pltpu.VMEM((rows, slot_total), BF16),
            pltpu.VMEM((low_rows, slot_total), BF16),
            pltpu.VMEM((slot_total, low_rows), BF16),
            weight_array, weight_array, weight_array,
            by_block, by_level,
            slot_array, slot_array, slot_array,
            slot_array, slot_array, slot_array,
            by_level, by_block,
            dma((4,)),
        ] + [dma((fields,))] * 12,
        compiler_params=pltpu.CompilerParams(
            vmem_limit_bytes=VMEM_LIMIT, collective_id=0, has_side_effects=True
        ),
    )(
        slots.reshape(1, rows), slots.reshape(rows, 1),
        lower.reshape(1, slot_total), lower.reshape(slot_total, 1),
        vertical_weight.reshape(rows, width), diffusion_inverse[0], cot, state,
    )
    tangent = tangent.reshape(1, levels, fields, per, width).transpose(0, 1, 3, 2, 4)
    adjoint = adjoint.reshape(1, here, fields, blocks, width).transpose(0, 1, 3, 2, 4)
    return tangent, adjoint


def solution(mesh):
    placed = (
        P("lat", "slab", None, None, None),
        P("lat", None, "slab", None, None),
        P("lat", "slab", None, None),
        P("lat", None, None, None),
        P("lat", "slab", None, None, None),
        P("lat", "slab", None),
    )
    return jax.shard_map(
        body,
        mesh=mesh,
        in_specs=placed,
        out_specs=(P("lat", None, "slab", None, None), P("lat", "slab", None, None, None)),
        check_vma=False,
    )
```

time: 494 us -> 153 us (0.31); the launches traced: 485 us -> 153 us
  waiting for transfers between devices: 287 us -> 0 us
  Pallas kernels: 0 us -> 145 us
  local copies, waits for them, and re-layouts: 105 us -> 7.71 us
  starting transfers between devices: 53.2 us -> 0 us
  matrix products: 33.3 us -> 0 us
  other arithmetic: 6.18 us -> 0 us
    all_to_all x6 -> x0, waiting for transfers between devices: 287 us -> none  [the longest x1 106 us: body(): lax.all_to_all(slot_back.reshape(lower_idx.shape + (2, fields, width)), '...]
    pallas_call x0 -> x1, Pallas kernels: none -> 145 us  [body(): pl.pallas_call(whole, out_shape=(jax.ShapeDtypeStruct((levels * fields *...]
    all_to_all x6 -> x0, starting transfers between devices: 53.2 us -> none  [the longest x1 12.8 us: body(): lax.all_to_all(lax.all_to_all(paired, 'lat', split_axis=0, concat_axis=0,...]
    reshape x8 -> x0, local copies, waits for them, and re-layouts: 51 us -> none  [the longest x2 16.4 us: body(): paired = paired.reshape(lower_idx.shape + (2, fields, width))]
    all_to_all x8 -> x0, local copies, waits for them, and re-layouts: 33.8 us -> none  [the longest x1 7.89 us: body(): lax.all_to_all(slot_back.reshape(lower_idx.shape + (2, fields, width)), '...]
    dot_general x6 -> x0, matrix products: 33.3 us -> none  [the longest x2 14 us: select(): jnp.dot(table, values, precision=lax.Precision.HIGHEST, preferred_element...]
    slice x6 -> x0, local copies, waits for them, and re-layouts: 7.69 us -> none  [the longest x2 3.93 us: body(): level_rows[blocks:]]
    dot_general x1 -> x0, local copies, waits for them, and re-layouts: 5.96 us -> none  [select(): jnp.dot(table, values, precision=lax.Precision.HIGHEST, preferred_element...]
  transfers between devices with their start and end apart: 6 -> 0, of which waited for: 4 -> 0; matrix products, arithmetic and copies ran while one was open for 27% -> 0% of each run, Pallas kernels for 0% -> 0%
where the time goes in v2:
time: 153 us
  Pallas kernels  145 us (95%)
  local copies, waits for them, and re-layouts  7.71 us (5%)
    pallas_call x1, Pallas kernels, body(): pl.pallas_call(whole, out_shape=(jax.ShapeDtypeStruct((levels * fields *...  145 us
    unnamed x5, local copies, waits for them, and re-layouts  4.49 us

profile of v2, /device:TPU:1, one launch (start us, length us, event | category | flops | bytes accessed | tf_op | source)
XLA Modules:
  0.0 153.2 jit_solution(1944617213907943098)
XLA Ops:
  0.6 0.8 copy.10
  1.5 0.7 reshape_reshape.14.lower_row
  2.2 1.5 %copy.12.slots_col = s32[512,1]{1,0:T(8,128)} copy(s32[512,1]{0,1:T(1,128)} %bitcast.26) | data formatting | bytes 4096 | tf_op jit(solution)/shard_map/reshape;reshape | solution.py:267
  3.7 1.0 reshape_reshape.16.lower_col
  4.7 144.9 %shard_map.77 = (f32[2560,128]{1,0:T(8,128)}, f32[4,5,128,128]{3,2,1,0:T(8,128)}) custom-call(s32[1,512]{1,0:T(1,128)} %bitcast.27, s32[512,1]{1,0:T(8,128)} %copy.12.slots_col, s32[1,1024]{1,0:T(1,128)} %reshape_reshape.14.lower_row, s32[1024,1]{1,0:T(8,128)} %reshape_reshape.16.lower_col, f32[512,128]{1,0:T(8,128)} %bitcast.25, f32[5,128,128]{2,1,0:T(8,128)} %bitcast.24, ...), custom_call_target="tpu_custom_call" | custom-call | tf_op jit(solution)/shard_map/pallas_call | solution.py:243
  149.6 0.0 copy-start
  149.6 2.6 %copy.16 = f32[1,128,4,5,128]{4,2,3,1,0:T(4,128)} copy(f32[1,128,4,5,128]{4,2,3,1,0:T(4,128)} %bitcast.23) | data formatting | bytes 2621440
  152.2 0.0 copy-done
  152.2 1.1 copy.17
Async XLA Ops:
  149.6 2.6 %copy-start = (f32[4,5,128,128]{3,2,1,0:T(8,128)S(1)}, f32[4,5,128,128]{3,2,1,0:T(8,128)}, u32[]{:S(2)}) copy-start(f32[4,5,128,128]{3,2,1,0:T(8,128)} %get-tuple-element.5) | copy-start | bytes 3932164

commit v3 on v2

--- a/solution.py
+++ b/solution.py
@@ -24,8 +24,17 @@
     return out[:, :width] + out[:, width:]
 
 
-def one_hot(shape, ids, axis):
-    return (lax.broadcasted_iota(jnp.int32, shape, axis) == ids).astype(F32).astype(BF16)
+def iota(shape, axis):
+    return lax.broadcasted_iota(jnp.int32, shape, axis)
+
+
+def slab_peer(s, t):
+    i = t + (t + 29) // 32
+    q, j = i % 4, (i // 4) % 4
+    dx = (q // 2) * (6 - 2 * q) + (1 - q // 2) * (1 + 2 * q)
+    dy = dx + j + (j // 2) * (1 - 2 * (j % 2))
+    x, y, core = s // 8, (s // 2) % 4, s % 2
+    return ((x + dx) % 4) * 8 + ((y + dy) % 4) * 2 + (core + i // 16) % 2
 
 
 def side_by_side(view, first, stride, per, levels):
@@ -44,10 +53,10 @@
         pl.semaphore_signal(bar, inc=1, device_id=((g + k) % n_lat, s), device_id_type=MESH)
 
     def one(k, carry):
-        pl.semaphore_signal(bar, inc=1, device_id=(g, (s + k) % n_slab), device_id_type=MESH)
+        pl.semaphore_signal(bar, inc=1, device_id=(g, slab_peer(s, k)), device_id_type=MESH)
         return carry
 
-    lax.fori_loop(1, n_slab, one, 0)
+    lax.fori_loop(0, n_slab - 1, one, 0)
 
 
 def wait_all(ref, sem):
@@ -55,12 +64,14 @@
 
 
 def whole(
-    slots_row, slots_col, lower_row, lower_col, weights, inverse, cot, state,
-    tangent, adjoint,
+    slots, lower, weights_in, inverse_in, cot_in, state_in,
+    tangent_out, adjoint_out,
+    weights, inverse, cot, state, tangent, adjoint,
     to_slot, from_slot, to_row, from_row,
     wx, wz, wo, bx, bk, fx, fz, fo, ax, ab, ao, mx, mo,
     w_sem, b_send, b_recv, fz_send, fz_recv, fx_send, fx_recv,
     az_send, az_recv, ax_send, ax_recv, m_send, m_recv,
+    in_sem, out_sem,
 ):
     g, s = lax.axis_index("lat"), lax.axis_index("slab")
     fields, n_lat, n_slab, cap = fx.shape[:4]
@@ -75,13 +86,13 @@
         pltpu.make_async_copy(source(s), target(s), recv).start()
 
         def one(k, carry):
-            peer = (s + k) % n_slab
+            peer = slab_peer(s, k)
             pltpu.make_async_remote_copy(
                 source(peer), target(s), send, recv, device_id=(g, peer), device_id_type=MESH
             ).start()
             return carry
 
-        lax.fori_loop(1, n_slab, one, 0)
+        lax.fori_loop(0, n_slab - 1, one, 0)
 
     def lat_sends(source, target, send, recv):
         pltpu.make_async_copy(source(g), target(g), recv).start()
@@ -100,8 +111,17 @@
     def at_field(f, count):
         return pl.ds(f * count, count)
 
+    inputs = [
+        pltpu.make_async_copy(a, b, in_sem.at[i])
+        for i, (a, b) in enumerate(
+            [(weights_in, weights), (inverse_in, inverse), (cot_in, cot), (state_in, state)]
+        )
+    ]
+    for copy in inputs:
+        copy.start()
     signal_peers(g, s, n_lat, n_slab)
-    to_slot[...] = one_hot((slot_total, rows), slots_row[...], 0)
+    to_slot[...] = (iota((slot_total, rows), 0) == slots[...]).astype(F32).astype(BF16)
+    inputs[0].wait()
     wx.reshape(slot_total, 128)[...] = pick(to_slot[...], weights[...])
     pl.semaphore_wait(pltpu.get_barrier_semaphore(), n_lat + n_slab - 2)
     lat_sends(lambda p: wx.at[p], lambda p: wz.at[p], w_sem.at[0], w_sem.at[1])
@@ -115,6 +135,8 @@
             preferred_element_type=F32,
         )
         lay_down(local_rows(bx), f * rows, per, per, levels, out)
+
+    def backward_slab(f):
         slab_sends(lambda p: bx.at[f, p], lambda p: bk.at[f, :, p], b_send.at[f], b_recv.at[f])
 
     def spread(f):
@@ -175,38 +197,68 @@
         for l in range(1, here - 1):
             adjoint[l, f] = low[l] + high[l - 1]
         adjoint[here - 1, f] = high[here - 2]
-
-    for f in range(fields):
+        pltpu.make_async_copy(adjoint.at[:, f], adjoint_out.at[:, f], out_sem.at[f]).start()
+
+    each = n_slab * cap
+
+    def row_table(p):
+        widen = (iota((each, n_slab), 0) // cap == iota((each, n_slab), 1)).astype(F32)
+        by_slot = lax.dot_general(
+            widen,
+            lower[p].astype(F32),
+            (((1,), (1,)), ((), ())),
+            precision=lax.Precision.HIGHEST,
+            preferred_element_type=F32,
+        )
+        here_only = iota((each, cap), 0) % cap == iota((each, cap), 1)
+        ids = jnp.sum(jnp.where(here_only, by_slot, 0.0), axis=1, keepdims=True).astype(jnp.int32)
+        return (iota((each, low_rows), 1) == ids).astype(F32)
+
+    inputs[1].wait()
+    inputs[2].wait()
+    backward(0)
+    backward_slab(0)
+    for p in range(n_lat):
+        from_row[p * each : (p + 1) * each, :] = row_table(p).astype(BF16)
+    spread(0)
+    for f in range(1, fields):
         backward(f)
-    from_row[...] = one_hot((slot_total, low_rows), lower_col[...], 1)
-    spread(0)
+    inputs[3].wait()
+    wait_all(wz, w_sem.at[1])
     lat_sends(lambda p: ax.at[0, p], lambda p: ab.at[0, p], az_send.at[0], az_recv.at[0])
-    wait_all(wz, w_sem.at[1])
     slab_sends(lambda p: wz.at[:, p], lambda p: wo.at[:, p], w_sem.at[2], w_sem.at[3])
-    spread(1)
+    for f in range(1, fields):
+        backward_slab(f)
     wait_all(wo, w_sem.at[3])
     for f in range(fields):
         gather(f)
+    spread(1)
+    adjoint_slab(1)
     wait_all(ab.at[0], az_recv.at[0])
     slab_sends(lambda p: ab.at[0, :, p], lambda p: ao.at[0, :, p], ax_send.at[0], ax_recv.at[0])
-    adjoint_slab(1)
     for f in range(2, fields):
         spread(f)
         adjoint_slab(f)
-    from_slot[...] = one_hot((rows, slot_total), slots_col[...], 1)
-    to_row[...] = one_hot((low_rows, slot_total), lower_row[...], 0)
+    for p in range(n_lat):
+        ids = iota((each, rows), 0) + p * each
+        from_slot[:, p * each : (p + 1) * each] = (ids == slots[...]).astype(F32).T.astype(BF16)
+        to_row[:, p * each : (p + 1) * each] = row_table(p).T.astype(BF16)
     for f in range(fields):
         pass_on(f)
-        if f == 0:
+        if f == 3:
             scatter(0, ax_recv.at[0])
+        if f < 2:
+            adjoint_lat(2 * f + 1)
+            adjoint_lat(2 * f + 2)
         if f >= 1:
-            adjoint_lat(f)
             arrive(f - 1)
         if f >= 2:
             finish(f - 2)
     arrive(fields - 1)
     finish(fields - 2)
     finish(fields - 1)
+    tangent_copy = pltpu.make_async_copy(tangent, tangent_out, out_sem.at[fields])
+    tangent_copy.start()
     for f in range(1, fields):
         scatter(f, az_recv.at[f])
 
@@ -219,6 +271,22 @@
         wait_all(mo.at[f, : n_slab - 1], m_send.at[f])
         wait_all(ao.at[f, : n_lat - 1], az_send.at[f])
         wait_all(ab.at[f, :, : n_slab - 1], ax_send.at[f])
+    tangent_copy.wait()
+    for f in range(fields):
+        pltpu.make_async_copy(adjoint.at[:, f], adjoint_out.at[:, f], out_sem.at[f]).wait()
+
+
+def settle(first_in, second_in, first_out, second_out, sems):
+    copies = []
+    for i, (a, b) in enumerate(((first_in, first_out), (second_in, second_out))):
+        for j in range(4):
+            part = a.shape[0] // 4
+            cut = pl.ds(j * part, part)
+            copies.append(pltpu.make_async_copy(a.at[cut], b.at[cut], sems.at[4 * i + j]))
+    for copy in copies:
+        copy.start()
+    for copy in copies:
+        copy.wait()
 
 
 def body(field_state, cotangent, vertical_weight, diffusion_inverse, source_row, dest_slot):
@@ -232,23 +300,30 @@
 
     state = field_state.transpose(0, 1, 3, 2, 4).reshape(here, fields, blocks, width)
     cot = cotangent.transpose(0, 1, 3, 2, 4).reshape(levels * fields * per, width)
-    lower = source_row.reshape(slot_total)
-    slots = dest_slot.reshape(rows)
+    lower = source_row.reshape(n_lat, n_slab, cap).transpose(0, 2, 1)
     vmem = pl.BlockSpec(memory_space=pltpu.VMEM)
+    anywhere = pl.BlockSpec(memory_space=pl.ANY)
     slot_array = pltpu.VMEM((fields, n_lat, n_slab, cap, width), F32)
     weight_array = pltpu.VMEM((n_lat, n_slab, cap, width), F32)
     by_level = pltpu.VMEM((fields, here, n_slab, per, width), F32)
     by_block = pltpu.VMEM((fields, n_slab, here, per, width), F32)
 
-    tangent, adjoint = pl.pallas_call(
+    shapes = (
+        jax.ShapeDtypeStruct((levels * fields * per, width), F32),
+        jax.ShapeDtypeStruct((here, fields, blocks, width), F32),
+    )
+    results = pl.pallas_call(
         whole,
-        out_shape=(
-            jax.ShapeDtypeStruct((levels * fields * per, width), F32),
-            jax.ShapeDtypeStruct((here, fields, blocks, width), F32),
-        ),
-        in_specs=[vmem] * 8,
-        out_specs=(vmem, vmem),
+        out_shape=shapes,
+        in_specs=[vmem] * 2 + [anywhere] * 4,
+        out_specs=(anywhere, anywhere),
         scratch_shapes=[
+            pltpu.VMEM((rows, width), F32),
+            pltpu.VMEM((fields, levels, levels), F32),
+            pltpu.VMEM((levels * fields * per, width), F32),
+            pltpu.VMEM((here, fields, blocks, width), F32),
+            pltpu.VMEM((levels * fields * per, width), F32),
+            pltpu.VMEM((here, fields, blocks, width), F32),
             pltpu.VMEM((slot_total, rows), BF16),
             pltpu.VMEM((rows, slot_total), BF16),
             pltpu.VMEM((low_rows, slot_total), BF16),
@@ -259,15 +334,15 @@
             slot_array, slot_array, slot_array,
             by_level, by_block,
             dma((4,)),
-        ] + [dma((fields,))] * 12,
+        ] + [dma((fields,))] * 12 + [dma((4,)), dma((fields + 1,))],
         compiler_params=pltpu.CompilerParams(
             vmem_limit_bytes=VMEM_LIMIT, collective_id=0, has_side_effects=True
         ),
     )(
-        slots.reshape(1, rows), slots.reshape(rows, 1),
-        lower.reshape(1, slot_total), lower.reshape(slot_total, 1),
+        dest_slot.reshape(1, rows), lower,
         vertical_weight.reshape(rows, width), diffusion_inverse[0], cot, state,
     )
+    tangent, adjoint = results
     tangent = tangent.reshape(1, levels, fields, per, width).transpose(0, 1, 3, 2, 4)
     adjoint = adjoint.reshape(1, here, fields, blocks, width).transpose(0, 1, 3, 2, 4)
     return tangent, adjoint

time: 153 us -> 148 us (0.967)
  local copies, waits for them, and re-layouts: 7.71 us -> 3.65 us
    another operation x3 -> x0, local copies, waits for them, and re-layouts: 3.22 us -> none  [the longest x1 1.53 us: body(): slots.reshape(rows, 1)]
    unnamed x5 -> x4, local copies, waits for them, and re-layouts: 4.49 us -> 3.65 us
where the time goes in v3:
time: 148 us
  Pallas kernels  144 us (97%)
  local copies, waits for them, and re-layouts  3.65 us (2%)
    pallas_call x1, Pallas kernels, body(): pl.pallas_call(whole, out_shape=shapes, in_specs=[vmem] * 2 + [anywhere]...  144 us
    unnamed x4, local copies, waits for them, and re-layouts  3.65 us

profile of v3, /device:TPU:1, one launch (start us, length us, event | category | flops | bytes accessed | tf_op | source)
XLA Modules:
  0.0 148.1 jit_solution(10992757601251390934)
XLA Ops:
  0.6 143.8 %shard_map.77 = (f32[2560,128]{1,0:T(8,128)}, f32[4,5,128,128]{3,2,1,0:T(8,128)}) custom-call(s32[1,512]{1,0:T(1,128)} %bitcast.25, s32[8,4,32]{2,1,0:T(4,128)} %bitcast.24, f32[512,128]{1,0:T(8,128)} %bitcast.23, f32[5,128,128]{2,1,0:T(8,128)} %bitcast.22, f32[2560,128]{1,0:T(8,128)} %bitcast.18, f32[4,5,128,128]{3,2,1,0:T(8,128)} %bitcast.19), custom_call_target="tpu_custom_call" | custom-call | tf_op jit(solution)/shard_map/pallas_call | solution.py:315
  144.4 0.0 copy-start
  144.4 2.6 %copy.10 = f32[1,128,4,5,128]{4,2,3,1,0:T(4,128)} copy(f32[1,128,4,5,128]{4,2,3,1,0:T(4,128)} %bitcast.21) | data formatting | bytes 2621440
  147.0 0.0 copy-done
  147.0 1.1 copy.11
Async XLA Ops:
  144.4 2.6 %copy-start = (f32[4,5,128,128]{3,2,1,0:T(8,128)S(1)}, f32[4,5,128,128]{3,2,1,0:T(8,128)}, u32[]{:S(2)}) copy-start(f32[4,5,128,128]{3,2,1,0:T(8,128)} %get-tuple-element.5) | copy-start | bytes 3932164

commit v4 on v3

--- a/solution.py
+++ b/solution.py
@@ -71,7 +71,7 @@
     wx, wz, wo, bx, bk, fx, fz, fo, ax, ab, ao, mx, mo,
     w_sem, b_send, b_recv, fz_send, fz_recv, fx_send, fx_recv,
     az_send, az_recv, ax_send, ax_recv, m_send, m_recv,
-    in_sem, out_sem,
+    in_sem, out_sem, last_recv,
 ):
     g, s = lax.axis_index("lat"), lax.axis_index("slab")
     fields, n_lat, n_slab, cap = fx.shape[:4]
@@ -117,14 +117,28 @@
             [(weights_in, weights), (inverse_in, inverse), (cot_in, cot), (state_in, state)]
         )
     ]
-    for copy in inputs:
+    inputs[0].start()
+    signal_peers(g, s, n_lat, n_slab)
+    for copy in inputs[1:]:
         copy.start()
-    signal_peers(g, s, n_lat, n_slab)
-    to_slot[...] = (iota((slot_total, rows), 0) == slots[...]).astype(F32).astype(BF16)
+    each = n_slab * cap
     inputs[0].wait()
-    wx.reshape(slot_total, 128)[...] = pick(to_slot[...], weights[...])
-    pl.semaphore_wait(pltpu.get_barrier_semaphore(), n_lat + n_slab - 2)
-    lat_sends(lambda p: wx.at[p], lambda p: wz.at[p], w_sem.at[0], w_sem.at[1])
+    weight_parts = jnp.concatenate(split(weights[...]), axis=1)
+    for k in (4, 1, 7, 2, 6, 3, 5, 0):
+        p = (g + k) % n_lat
+        here_rows = pl.ds(pl.multiple_of(p * each, each), each)
+        table = (iota((each, rows), 0) + p * each == slots[...]).astype(F32).astype(BF16)
+        to_slot[here_rows, :] = table
+        out = jnp.dot(table, weight_parts, preferred_element_type=F32)
+        wx.reshape(slot_total, 128)[here_rows, :] = out[:, :128] + out[:, 128:]
+        if k == 4:
+            pl.semaphore_wait(pltpu.get_barrier_semaphore(), n_lat + n_slab - 2)
+        if k == 0:
+            pltpu.make_async_copy(wx.at[p], wz.at[p], w_sem.at[1]).start()
+        else:
+            pltpu.make_async_remote_copy(
+                wx.at[p], wz.at[g], w_sem.at[0], w_sem.at[1], device_id=(p, s), device_id_type=MESH
+            ).start()
 
     def backward(f):
         out = lax.dot_general(
@@ -184,13 +198,31 @@
 
     def adjoint_lat(f):
         wait_all(ab.at[f], ax_recv.at[f])
-        lat_sends(lambda p: ab.at[f, p], lambda p: ao.at[f, p], az_send.at[f], az_recv.at[f])
+        recv = last_recv.at[g] if f == fields - 1 else az_recv.at[f]
+        lat_sends(lambda p: ab.at[f, p], lambda p: ao.at[f, p], az_send.at[f], recv)
+
+    def contributions(table, row, part):
+        return pick(table, jnp.concatenate([(1.0 - part) * row, part * row], axis=1))
 
     def scatter(f, sem):
         wait_all(ao.at[f], sem)
         row = slot_rows(ao)[at_field(f, slot_total), :]
-        part = wo.reshape(slot_total, 128)[...]
-        both = pick(to_row[...], jnp.concatenate([(1.0 - part) * row, part * row], axis=1))
+        put(f, contributions(to_row[...], row, wo.reshape(slot_total, 128)[...]))
+
+    def scatter_last(f):
+        both = jnp.zeros((low_rows, 256), F32)
+        for k in (0, 1, 7, 2, 6, 3, 5, 4):
+            p = (g + k) % n_lat
+            wait_all(ao.at[f, p], last_recv.at[p])
+            first = pl.multiple_of(p * each, each)
+            both += contributions(
+                to_row[:, pl.ds(first, each)],
+                slot_rows(ao)[pl.ds(f * slot_total + first, each), :],
+                wo.reshape(slot_total, 128)[pl.ds(first, each), :],
+            )
+        put(f, both)
+
+    def put(f, both):
         low = both[:, :128].reshape(here - 1, blocks, 128)
         high = both[:, 128:].reshape(here - 1, blocks, 128)
         adjoint[0, f] = low[0]
@@ -198,8 +230,6 @@
             adjoint[l, f] = low[l] + high[l - 1]
         adjoint[here - 1, f] = high[here - 2]
         pltpu.make_async_copy(adjoint.at[:, f], adjoint_out.at[:, f], out_sem.at[f]).start()
-
-    each = n_slab * cap
 
     def row_table(p):
         widen = (iota((each, n_slab), 0) // cap == iota((each, n_slab), 1)).astype(F32)
@@ -214,53 +244,66 @@
         ids = jnp.sum(jnp.where(here_only, by_slot, 0.0), axis=1, keepdims=True).astype(jnp.int32)
         return (iota((each, low_rows), 1) == ids).astype(F32)
 
+    early = 2
+
+    def early_lat(f):
+        lat_sends(lambda p: ax.at[f, p], lambda p: ab.at[f, p], az_send.at[f], az_recv.at[f])
+
+    def early_slab(f):
+        wait_all(ab.at[f], az_recv.at[f])
+        slab_sends(lambda p: ab.at[f, :, p], lambda p: ao.at[f, :, p], ax_send.at[f], ax_recv.at[f])
+
     inputs[1].wait()
     inputs[2].wait()
-    backward(0)
-    backward_slab(0)
+    for f in range(early):
+        backward(f)
+        backward_slab(f)
     for p in range(n_lat):
         from_row[p * each : (p + 1) * each, :] = row_table(p).astype(BF16)
     spread(0)
-    for f in range(1, fields):
+    early_lat(0)
+    for f in range(1, early):
+        spread(f)
+    for f in range(early, fields):
         backward(f)
     inputs[3].wait()
     wait_all(wz, w_sem.at[1])
-    lat_sends(lambda p: ax.at[0, p], lambda p: ab.at[0, p], az_send.at[0], az_recv.at[0])
     slab_sends(lambda p: wz.at[:, p], lambda p: wo.at[:, p], w_sem.at[2], w_sem.at[3])
-    for f in range(1, fields):
+    for f in range(1, early):
+        early_lat(f)
+    for f in range(early, fields):
         backward_slab(f)
     wait_all(wo, w_sem.at[3])
     for f in range(fields):
         gather(f)
-    spread(1)
-    adjoint_slab(1)
-    wait_all(ab.at[0], az_recv.at[0])
-    slab_sends(lambda p: ab.at[0, :, p], lambda p: ao.at[0, :, p], ax_send.at[0], ax_recv.at[0])
-    for f in range(2, fields):
+    early_slab(0)
+    for f in range(early, fields):
         spread(f)
         adjoint_slab(f)
+    for f in range(1, early):
+        early_slab(f)
     for p in range(n_lat):
         ids = iota((each, rows), 0) + p * each
         from_slot[:, p * each : (p + 1) * each] = (ids == slots[...]).astype(F32).T.astype(BF16)
         to_row[:, p * each : (p + 1) * each] = row_table(p).T.astype(BF16)
     for f in range(fields):
         pass_on(f)
-        if f == 3:
-            scatter(0, ax_recv.at[0])
-        if f < 2:
-            adjoint_lat(2 * f + 1)
-            adjoint_lat(2 * f + 2)
+        if f < fields - early:
+            adjoint_lat(early + f)
         if f >= 1:
             arrive(f - 1)
         if f >= 2:
             finish(f - 2)
+        if f >= fields - early:
+            scatter(f - fields + early, ax_recv.at[f - fields + early])
     arrive(fields - 1)
     finish(fields - 2)
     finish(fields - 1)
     tangent_copy = pltpu.make_async_copy(tangent, tangent_out, out_sem.at[fields])
     tangent_copy.start()
-    for f in range(1, fields):
+    for f in range(early, fields - 1):
         scatter(f, az_recv.at[f])
+    scatter_last(fields - 1)
 
     wait_all(wz.at[: n_lat - 1], w_sem.at[0])
     wait_all(wo.at[:, : n_slab - 1], w_sem.at[2])
@@ -274,19 +317,6 @@
     tangent_copy.wait()
     for f in range(fields):
         pltpu.make_async_copy(adjoint.at[:, f], adjoint_out.at[:, f], out_sem.at[f]).wait()
-
-
-def settle(first_in, second_in, first_out, second_out, sems):
-    copies = []
-    for i, (a, b) in enumerate(((first_in, first_out), (second_in, second_out))):
-        for j in range(4):
-            part = a.shape[0] // 4
-            cut = pl.ds(j * part, part)
-            copies.append(pltpu.make_async_copy(a.at[cut], b.at[cut], sems.at[4 * i + j]))
-    for copy in copies:
-        copy.start()
-    for copy in copies:
-        copy.wait()
 
 
 def body(field_state, cotangent, vertical_weight, diffusion_inverse, source_row, dest_slot):
@@ -334,7 +364,7 @@
             slot_array, slot_array, slot_array,
             by_level, by_block,
             dma((4,)),
-        ] + [dma((fields,))] * 12 + [dma((4,)), dma((fields + 1,))],
+        ] + [dma((fields,))] * 12 + [dma((4,)), dma((fields + 1,)), dma((n_lat,))],
         compiler_params=pltpu.CompilerParams(
             vmem_limit_bytes=VMEM_LIMIT, collective_id=0, has_side_effects=True
         ),

time: 148 us -> 146 us (0.986)
  Pallas kernels: 144 us -> 142 us
    pallas_call x1, Pallas kernels: 144 us -> 142 us  [body(): pl.pallas_call(whole, out_shape=shapes, in_specs=[vmem] * 2 + [anywhere]...]
where the time goes in v4:
time: 146 us
  Pallas kernels  142 us (97%)
  local copies, waits for them, and re-layouts  3.65 us (2%)
    pallas_call x1, Pallas kernels, body(): pl.pallas_call(whole, out_shape=shapes, in_specs=[vmem] * 2 + [anywhere]...  142 us
    unnamed x4, local copies, waits for them, and re-layouts  3.65 us

profile of v4, /device:TPU:1, one launch (start us, length us, event | category | flops | bytes accessed | tf_op | source)
XLA Modules:
  0.0 146.3 jit_solution(9382010997632992977)
XLA Ops:
  0.6 142.0 %shard_map.77 = (f32[2560,128]{1,0:T(8,128)}, f32[4,5,128,128]{3,2,1,0:T(8,128)}) custom-call(s32[1,512]{1,0:T(1,128)} %bitcast.25, s32[8,4,32]{2,1,0:T(4,128)} %bitcast.24, f32[512,128]{1,0:T(8,128)} %bitcast.23, f32[5,128,128]{2,1,0:T(8,128)} %bitcast.22, f32[2560,128]{1,0:T(8,128)} %bitcast.18, f32[4,5,128,128]{3,2,1,0:T(8,128)} %bitcast.19), custom_call_target="tpu_custom_call" | custom-call | tf_op jit(solution)/shard_map/pallas_call | solution.py:345
  142.6 0.0 copy-start
  142.6 2.6 %copy.10 = f32[1,128,4,5,128]{4,2,3,1,0:T(4,128)} copy(f32[1,128,4,5,128]{4,2,3,1,0:T(4,128)} %bitcast.21) | data formatting | bytes 2621440
  145.2 0.0 copy-done
  145.2 1.1 copy.11
Async XLA Ops:
  142.6 2.6 %copy-start = (f32[4,5,128,128]{3,2,1,0:T(8,128)S(1)}, f32[4,5,128,128]{3,2,1,0:T(8,128)}, u32[]{:S(2)}) copy-start(f32[4,5,128,128]{3,2,1,0:T(8,128)} %get-tuple-element.5) | copy-start | bytes 3932164

commit v5 on v4

--- a/solution.py
+++ b/solution.py
@@ -8,7 +8,7 @@
 from jax.sharding import PartitionSpec as P
 
 MESH = pl.DeviceIdType.MESH
-VMEM_LIMIT = 60 << 20
+VMEM_LIMIT = 40 << 20
 F32 = jnp.float32
 BF16 = jnp.bfloat16
 
@@ -64,9 +64,9 @@
 
 
 def whole(
-    slots, lower, weights_in, inverse_in, cot_in, state_in,
+    slots_in, lower_in, weights_in, inverse_in, cot_in, state_in,
     tangent_out, adjoint_out,
-    weights, inverse, cot, state, tangent, adjoint,
+    slots, lower, weights, inverse, cot, state, tangent, adjoint,
     to_slot, from_slot, to_row, from_row,
     wx, wz, wo, bx, bk, fx, fz, fo, ax, ab, ao, mx, mo,
     w_sem, b_send, b_recv, fz_send, fz_recv, fx_send, fx_recv,
@@ -114,14 +114,19 @@
     inputs = [
         pltpu.make_async_copy(a, b, in_sem.at[i])
         for i, (a, b) in enumerate(
-            [(weights_in, weights), (inverse_in, inverse), (cot_in, cot), (state_in, state)]
+            [
+                (weights_in, weights), (inverse_in, inverse), (cot_in, cot), (state_in, state),
+                (slots_in, slots), (lower_in, lower),
+            ]
         )
     ]
+    inputs[4].start()
     inputs[0].start()
     signal_peers(g, s, n_lat, n_slab)
-    for copy in inputs[1:]:
-        copy.start()
+    for i in (1, 2, 5, 3):
+        inputs[i].start()
     each = n_slab * cap
+    inputs[4].wait()
     inputs[0].wait()
     weight_parts = jnp.concatenate(split(weights[...]), axis=1)
     for k in (4, 1, 7, 2, 6, 3, 5, 0):
@@ -255,6 +260,7 @@
 
     inputs[1].wait()
     inputs[2].wait()
+    inputs[5].wait()
     for f in range(early):
         backward(f)
         backward_slab(f)
@@ -331,7 +337,6 @@
     state = field_state.transpose(0, 1, 3, 2, 4).reshape(here, fields, blocks, width)
     cot = cotangent.transpose(0, 1, 3, 2, 4).reshape(levels * fields * per, width)
     lower = source_row.reshape(n_lat, n_slab, cap).transpose(0, 2, 1)
-    vmem = pl.BlockSpec(memory_space=pltpu.VMEM)
     anywhere = pl.BlockSpec(memory_space=pl.ANY)
     slot_array = pltpu.VMEM((fields, n_lat, n_slab, cap, width), F32)
     weight_array = pltpu.VMEM((n_lat, n_slab, cap, width), F32)
@@ -345,9 +350,11 @@
     results = pl.pallas_call(
         whole,
         out_shape=shapes,
-        in_specs=[vmem] * 2 + [anywhere] * 4,
+        in_specs=[anywhere] * 6,
         out_specs=(anywhere, anywhere),
         scratch_shapes=[
+            pltpu.VMEM((1, rows), jnp.int32),
+            pltpu.VMEM((n_lat, cap, n_slab), jnp.int32),
             pltpu.VMEM((rows, width), F32),
             pltpu.VMEM((fields, levels, levels), F32),
             pltpu.VMEM((levels * fields * per, width), F32),
@@ -364,13 +371,18 @@
             slot_array, slot_array, slot_array,
             by_level, by_block,
             dma((4,)),
-        ] + [dma((fields,))] * 12 + [dma((4,)), dma((fields + 1,)), dma((n_lat,))],
+        ] + [dma((fields,))] * 12 + [dma((6,)), dma((fields + 1,)), dma((n_lat,))],
         compiler_params=pltpu.CompilerParams(
             vmem_limit_bytes=VMEM_LIMIT, collective_id=0, has_side_effects=True
         ),
     )(
-        dest_slot.reshape(1, rows), lower,
-        vertical_weight.reshape(rows, width), diffusion_inverse[0], cot, state,
+        *(
+            pltpu.with_memory_space_constraint(part, pltpu.HBM)
+            for part in (
+                dest_slot.reshape(1, rows), lower,
+                vertical_weight.reshape(rows, width), diffusion_inverse[0], cot, state,
+            )
+        )
     )
     tangent, adjoint = results
     tangent = tangent.reshape(1, levels, fields, per, width).transpose(0, 1, 3, 2, 4)

time: 146 us -> 142 us (0.973)
  Pallas kernels: 142 us -> 138 us
  local copies, waits for them, and re-layouts: 3.65 us -> 2.11 us
    pallas_call x1, Pallas kernels: 142 us -> 138 us  [body(): pl.pallas_call(whole, out_shape=shapes, in_specs=[anywhere] * 6, out_spec...]
    unnamed x4 -> x2, local copies, waits for them, and re-layouts: 3.65 us -> 2.11 us
where the time goes in v5:
time: 142 us; the launch traced here: 141 us
  Pallas kernels  138 us (97%)
  local copies, waits for them, and re-layouts  2.11 us (1%)
    pallas_call x1, Pallas kernels, body(): pl.pallas_call(whole, out_shape=shapes, in_specs=[anywhere] * 6, out_spec...  138 us

profile of v5, /device:TPU:1, one launch (start us, length us, event | category | flops | bytes accessed | tf_op | source)
XLA Modules:
  0.0 141.0 jit_solution(7118069443204974208)
XLA Ops:
  0.6 138.2 %shard_map.77 = (f32[2560,128]{1,0:T(8,128)S(1)}, f32[4,5,128,128]{3,2,1,0:T(8,128)S(1)}) custom-call(s32[1,512]{1,0:T(1,128)} %bitcast.25, s32[8,4,32]{2,1,0:T(4,128)} %bitcast.24, f32[512,128]{1,0:T(8,128)} %bitcast.23, f32[5,128,128]{2,1,0:T(8,128)} %bitcast.22, f32[2560,128]{1,0:T(8,128)} %bitcast.20, f32[4,5,128,128]{3,2,1,0:T(8,128)} %bitcast.21), custom_call_target="tpu_custom_call" | custom-call | tf_op jit(solution)/shard_map/pallas_call | solution.py:350
  138.9 1.1 copy.10
  139.9 1.1 copy.11

commit v6 on v5

--- a/solution.py
+++ b/solution.py
@@ -309,8 +309,6 @@
     tangent_copy.start()
     for f in range(early, fields - 1):
         scatter(f, az_recv.at[f])
-    scatter_last(fields - 1)
-
     wait_all(wz.at[: n_lat - 1], w_sem.at[0])
     wait_all(wo.at[:, : n_slab - 1], w_sem.at[2])
     for f in range(fields):
@@ -318,9 +316,12 @@
         wait_all(fz.at[f, : n_lat - 1], fz_send.at[f])
         wait_all(fo.at[f, :, : n_slab - 1], fx_send.at[f])
         wait_all(mo.at[f, : n_slab - 1], m_send.at[f])
-        wait_all(ao.at[f, : n_lat - 1], az_send.at[f])
+        if f < fields - 1:
+            wait_all(ao.at[f, : n_lat - 1], az_send.at[f])
         wait_all(ab.at[f, :, : n_slab - 1], ax_send.at[f])
     tangent_copy.wait()
+    scatter_last(fields - 1)
+    wait_all(ao.at[fields - 1, : n_lat - 1], az_send.at[fields - 1])
     for f in range(fields):
         pltpu.make_async_copy(adjoint.at[:, f], adjoint_out.at[:, f], out_sem.at[f]).wait()
 

time: 142 us -> 142 us (level)
  no operation moved by 1% of the time
where the time goes in v6:
time: 142 us; the launch traced here: 141 us
  Pallas kernels  138 us (97%)
  local copies, waits for them, and re-layouts  2.11 us (1%)
    pallas_call x1, Pallas kernels, body(): pl.pallas_call(whole, out_shape=shapes, in_specs=[anywhere] * 6, out_spec...  138 us

profile of v6, /device:TPU:1, one launch (start us, length us, event | category | flops | bytes accessed | tf_op | source)
XLA Modules:
  0.0 140.9 jit_solution(16544459033430188786)
XLA Ops:
  0.6 138.2 %shard_map.77 = (f32[2560,128]{1,0:T(8,128)S(1)}, f32[4,5,128,128]{3,2,1,0:T(8,128)S(1)}) custom-call(s32[1,512]{1,0:T(1,128)} %bitcast.25, s32[8,4,32]{2,1,0:T(4,128)} %bitcast.24, f32[512,128]{1,0:T(8,128)} %bitcast.23, f32[5,128,128]{2,1,0:T(8,128)} %bitcast.22, f32[2560,128]{1,0:T(8,128)} %bitcast.20, f32[4,5,128,128]{3,2,1,0:T(8,128)} %bitcast.21), custom_call_target="tpu_custom_call" | custom-call | tf_op jit(solution)/shard_map/pallas_call | solution.py:351
  138.8 1.1 copy.10
  139.9 1.1 copy.11
